TPU v7x, 32 devices: a whole 2x2x4 slice. The times are simulated.
32 devices in a mesh: lon: 8 (over y, x, core), lat: 4 (over z).
Axes of the slice: x: 2, y: 2, z: 4, core: 2. Of those that a mesh axis runs over, the one named last changes fastest.
Arguments:
- ocean_state: float32 [4, 4, 512, 8192], P(None, None, 'lat', 'lon'), may hold values from -3 to 3
- depth_levels: int32 [512, 8192], P('lat', 'lon'), may hold values from 0 to 4
- vert_mix: float32 [4, 512, 8192], P(None, 'lat', 'lon'), may hold values from 0.1 to 4
- partner: int32 [8192], P('lon'), may hold values from 0 to 8191, as said below
- ice_velocity: float32 [2, 512, 8192], P(None, 'lat', 'lon'), may hold values from -4 to 4
- ice_mass: float32 [512, 8192], P('lat', 'lon'), may hold values from 0.2 to 2
- ice_strength: float32 [512, 8192], P('lat', 'lon'), may hold values from 0.2 to 2
- ice_mask: int32 [512, 8192], P('lat', 'lon'), may hold values 0 or 1
- ice_owned: int32 [4, 8, 3], P('lat', 'lon'), may hold values from -1 to 63, as said below
Outputs:
- new_tracers: float32 [2, 4, 512, 8192], P(None, None, 'lat', 'lon')
- new_ice_velocity: float32 [2, 512, 8192], P(None, 'lat', 'lon')
Inputs may be any that keep to these rules, and one draw needn't show every extreme that they name: partner[i] = (s - i) mod 8192 for one s drawn afresh; the partner of a column's partner is the column itself. `ice_owned`: entry [r, d, k] is -1 or a tile column of tile row r that lies on lon index (d - k) mod 8, that is, one of the 8 tile columns from ((d - k) mod 8) * 8 on; each tile column appears at most once in a row; in every row some lon index has all 3 slots filled and some lon index has none.
All inputs are finite; a program needn't handle non-finite values. No bound on the sum of `ice_mask` on one device may be relied on, other than what follows from the above.
Results may differ from a plain program's by a relative error of at most 0.0003.
Values sent between devices are 32-bit elements; how exact they have to be, the bound alone decides.
No kernel may reach another device: no remote copies, remote signals or barrier semaphores. Data moves between devices by JAX's collectives and lax.ppermute only.
A program may use at most 192 MiB of HBM per device.

v0:
```python
import functools

import jax
import jax.numpy as jnp
from jax import lax
from jax.experimental import pallas as pl
from jax.experimental.pallas import tpu as pltpu
from jax.sharding import PartitionSpec as P

TILE = 128
SUBCYCLES = 32
LANES = 128
SUB = 8

TIME_STEP = 0.25
MIX_HORIZ = 0.5
RELAX_RATE = 0.5
ECC_FACTOR = 0.25
DELTA_FLOOR_SQ = 0.25
INV_ICE_STEP = 2.0
WATER_DRAG = 1.0
CORIOLIS_PARAM = 0.5

f32 = jnp.float32
ANY = pl.BlockSpec(memory_space=pl.ANY)
SMEM_SPEC = pl.BlockSpec(memory_space=pltpu.SMEM)


def lane_ids():
    return lax.broadcasted_iota(jnp.int32, (SUB, LANES), 1)


def sub_ids():
    return lax.broadcasted_iota(jnp.int32, (SUB, LANES), 0)


def east_of(cur, nxt, lane0):
    return pltpu.roll(jnp.where(lane0, nxt, cur), LANES - 1, 1)


def west_of(cur, prev, lane_last):
    return pltpu.roll(jnp.where(lane_last, prev, cur), 1, 1)


def north_of(cur, nxt, sub0):
    return pltpu.roll(jnp.where(sub0, nxt, cur), SUB - 1, 0)


def south_of(cur, prev, sub_last):
    return pltpu.roll(jnp.where(sub_last, prev, cur), 1, 0)


N_VEC = TILE // SUB


def ice_tile(fields, mask_ref, depth_ref, st, cf):
    lane, sub = lane_ids(), sub_ids()
    lane_first, lane_last = lane == 0, lane == LANES - 1
    sub_first, sub_last = sub == 0, sub == SUB - 1
    zero = jnp.zeros((SUB, LANES), f32)

    def rows(ref, index, v):
        return ref[index, pl.ds(v, SUB, stride=N_VEC), :]

    def ahead_lane(x):
        return jnp.where(lane_last, zero, pltpu.roll(x, LANES - 1, 1))

    def behind_lane(x):
        return jnp.where(lane_first, zero, pltpu.roll(x, 1, 1))

    def ahead_wrap(x):
        return jnp.where(sub_last, zero, pltpu.roll(x, SUB - 1, 0))

    def behind_wrap(x):
        return jnp.where(sub_first, zero, pltpu.roll(x, 1, 0))

    half_p = []
    for v in range(N_VEC):
        ice = mask_ref[pl.ds(v, SUB, stride=N_VEC), :].astype(f32)
        wet = depth_ref[pl.ds(v, SUB, stride=N_VEC), :] > 0
        cover = jnp.where(wet, ice, zero)
        mass = rows(fields, 2, v) * cover
        strength = rows(fields, 3, v) * cover
        inertia = mass * INV_ICE_STEP
        diag = inertia + WATER_DRAG
        turn = CORIOLIS_PARAM * mass
        inv = 1.0 / (diag * diag + turn * turn)
        half = 0.5 * strength
        half_p.append(half)
        st[0, v] = rows(fields, 0, v)
        st[1, v] = rows(fields, 1, v)
        st[2, v] = half
        st[3, v] = half
        st[4, v] = zero
        cf[0, v] = strength * (1.0 / 12.0)
        cf[1, v] = inertia
        cf[2, v] = diag * inv
        cf[3, v] = turn * inv
    for v in range(N_VEC):
        half = half_p[v]
        below = half_p[v - 1] if v else behind_wrap(half_p[N_VEC - 1])
        cf[4, v] = WATER_DRAG * rows(fields, 4, v) - (half - behind_lane(half))
        cf[5, v] = WATER_DRAG * rows(fields, 5, v) - (half - below)

    keep = 1.0 / (1.0 + RELAX_RATE)

    def one_cycle(_, carry):
        def update(v, u, w, sxx, syy, s12, syy_below, s12_below):
            fx = (sxx - behind_lane(sxx)) + (s12 - s12_below)
            fy = (s12 - behind_lane(s12)) + (syy - syy_below)
            inertia, ca, cb = cf[1, v], cf[2, v], cf[3, v]
            rx = inertia * u + (fx + cf[4, v])
            ry = inertia * w + (fy + cf[5, v])
            st[0, v] = ca * rx + cb * ry
            st[1, v] = ca * ry - cb * rx

        u, w = st[0, 0], st[1, 0]
        first_u, first_w = u, w
        first = prev = None
        for v in range(N_VEC):
            if v + 1 < N_VEC:
                u_north, w_north = st[0, v + 1], st[1, v + 1]
            else:
                u_north, w_north = ahead_wrap(first_u), ahead_wrap(first_w)
            ux = ahead_lane(u) - u
            vy = w_north - w
            shear = (u_north - u) + (ahead_lane(w) - w)
            div = ux + vy
            tens = ux - vy
            div2 = div + div
            four = div2 * div2 + (tens * tens + (shear * shear + 4.0 * DELTA_FLOOR_SQ))
            k = cf[0, v] * lax.rsqrt(four)
            div4 = div2 + div2
            sxx = keep * st[2, v] + k * (div4 + tens)
            syy = keep * st[3, v] + k * (div4 - tens)
            s12 = keep * st[4, v] + (k + k) * shear
            st[2, v] = sxx
            st[3, v] = syy
            st[4, v] = s12
            if v == 0:
                first = (sxx, syy, s12)
            else:
                update(v, u, w, sxx, syy, s12, prev[1], prev[2])
            prev = (sxx, syy, s12)
            u, w = u_north, w_north
        update(0, first_u, first_w, *first, behind_wrap(prev[1]), behind_wrap(prev[2]))
        return carry

    lax.fori_loop(0, SUBCYCLES, one_cycle, 0)
    for v in range(N_VEC):
        fields[0, pl.ds(v, SUB, stride=N_VEC), :] = st[0, v]
        fields[1, pl.ds(v, SUB, stride=N_VEC), :] = st[1, v]


def tile_copies(col, refs, fields, mask_v, depth_v, sems):
    vel, mass, strength, mask, depth, ocean = refs
    levels = ocean.shape[0] // 4
    cols = pl.ds(pl.multiple_of(col * TILE, TILE), TILE)
    return [
        pltpu.make_async_copy(vel.at[:, :, cols], fields.at[0:2], sems.at[0]),
        pltpu.make_async_copy(mass.at[:, cols], fields.at[2], sems.at[1]),
        pltpu.make_async_copy(strength.at[:, cols], fields.at[3], sems.at[2]),
        pltpu.make_async_copy(ocean.at[2 * levels, :, cols], fields.at[4], sems.at[3]),
        pltpu.make_async_copy(ocean.at[3 * levels, :, cols], fields.at[5], sems.at[4]),
        pltpu.make_async_copy(mask.at[:, cols], mask_v, sems.at[5]),
        pltpu.make_async_copy(depth.at[:, cols], depth_v, sems.at[6]),
    ]


TILE_COPIES = 7


def ice_scratch():
    return [
        pltpu.VMEM((6, TILE, TILE), f32),
        pltpu.VMEM((TILE, TILE), jnp.int32),
        pltpu.VMEM((TILE, TILE), jnp.int32),
        pltpu.SemaphoreType.DMA((TILE_COPIES,)),
    ]


def first_ice_kernel(
    owned, vel, mass, strength, mask, depth, ocean, out,
    fields, mask_v, depth_v, sems, st, cf, all_vel, copy_sems, all_sem,
):
    tiles_dev = vel.shape[2] // TILE
    column = owned[0, 0, 0]
    listed = column >= 0
    local = jnp.where(listed, column - lax.axis_index("lon") * tiles_dev, -1)
    safe = jnp.clip(local, 0, tiles_dev - 1)
    refs = (vel, mass, strength, mask, depth, ocean)
    whole = pltpu.make_async_copy(vel, all_vel, all_sem)

    def pass_through(q):
        cols = pl.ds(q * TILE, TILE)
        return pltpu.make_async_copy(all_vel.at[:, :, cols], out.at[:, :, cols], copy_sems.at[q])

    @pl.when(listed)
    def _():
        for copy in tile_copies(safe, refs, fields, mask_v, depth_v, sems):
            copy.start()

    whole.start()
    whole.wait()
    for q in range(tiles_dev):

        @pl.when(local != q)
        def _():
            pass_through(q).start()

    @pl.when(listed)
    def _():
        for copy in tile_copies(safe, refs, fields, mask_v, depth_v, sems):
            copy.wait()
        ice_tile(fields, mask_v, depth_v, st, cf)
        cols = pl.ds(pl.multiple_of(safe * TILE, TILE), TILE)
        back = pltpu.make_async_copy(fields.at[0:2], out.at[:, :, cols], sems.at[0])
        back.start()
        back.wait()

    for q in range(tiles_dev):

        @pl.when(local != q)
        def _():
            pass_through(q).wait()


def first_ice(owned, vel, mass, strength, mask, depth, ocean):
    return pl.pallas_call(
        first_ice_kernel,
        out_shape=jax.ShapeDtypeStruct(vel.shape, f32),
        in_specs=[SMEM_SPEC] + [ANY] * 6,
        out_specs=ANY,
        scratch_shapes=ice_scratch()
        + [
            pltpu.VMEM((5, N_VEC, SUB, LANES), f32),
            pltpu.VMEM((6, N_VEC, SUB, LANES), f32),
            pltpu.VMEM(vel.shape, f32),
            pltpu.SemaphoreType.DMA((vel.shape[2] // TILE,)),
            pltpu.SemaphoreType.DMA,
        ],
        name="ice_first",
    )(owned, vel, mass, strength, mask, depth, ocean)


class Layout:
    def __init__(self, ocean, rows, cols):
        self.levels = ocean // 4
        self.planes = 2 * self.levels
        self.tiles = cols // LANES
        self.fold_depth = self.tiles * self.planes
        self.columns = self.fold_depth + self.tiles
        self.column_fields = self.planes + self.levels + 1
        self.owned = self.columns + 16
        self.size = self.owned + SUB
        self.row_fields = 16


def pack_kernel(
    lay, owned, ocean, depth, piece_out, up_out, down_out, top, top_d, bot, bot_d, west, west_d, east, east_d, tmp, sems
):
    planes, levels, tiles = lay.planes, lay.levels, lay.tiles
    rows, cols = ocean.shape[1], ocean.shape[2]
    n_lon = piece_out.shape[0]
    me = lax.axis_index("lon")
    last = pl.ds(rows - SUB, SUB)
    copies = [
        pltpu.make_async_copy(ocean.at[0:planes, :, 0:LANES], west, sems.at[0]),
        pltpu.make_async_copy(ocean.at[0 : planes + levels, :, cols - LANES : cols], east, sems.at[1]),
        pltpu.make_async_copy(depth.at[:, 0:LANES], west_d, sems.at[2]),
        pltpu.make_async_copy(depth.at[:, cols - LANES : cols], east_d, sems.at[3]),
        pltpu.make_async_copy(ocean.at[:, last, :], top, sems.at[4]),
        pltpu.make_async_copy(depth.at[last, :], top_d, sems.at[5]),
        pltpu.make_async_copy(ocean.at[0:planes, 0:SUB, :], bot, sems.at[6]),
        pltpu.make_async_copy(depth.at[0:SUB, :], bot_d, sems.at[7]),
    ]
    for copy in copies:
        copy.start()
    for copy in copies[:4]:
        copy.wait()
    lane = lane_ids()
    for v in range(rows // SUB):
        at = pl.ds(v * SUB, SUB)
        mixed = jnp.zeros((SUB, LANES), f32)
        for f in range(planes + levels + 1):
            block = east[f, at, :] if f < planes + levels else east_d[at, :].astype(f32)
            mixed = jnp.where(lane == f, pltpu.roll(block, (f + 1) % LANES, 1), mixed)
        for f in range(planes + 1):
            block = west[f, at, :] if f < planes else west_d[at, :].astype(f32)
            mixed = jnp.where(lane == 16 + f, pltpu.roll(block, 16 + f, 1), mixed)
        tmp[at, :] = mixed
    turned = jnp.transpose(tmp[...])
    east_rows, west_rows = turned[0:16], turned[16:32]
    own = jnp.zeros((SUB, LANES), f32)
    for slot in range(owned.shape[2]):
        own = jnp.where(lane == slot, owned[0, 0, slot].astype(f32), own)
    for copy in copies[4:]:
        copy.wait()
    top_rows = jnp.concatenate([top[p, SUB - 1 : SUB, :] for p in range(planes)], axis=0)
    bot_rows = jnp.concatenate([bot[p, 0:1, :] for p in range(planes)], axis=0)
    top_depth = top_d[SUB - 1 : SUB, :].astype(f32)
    up_out[0:planes, :] = top_rows
    for level in range(levels):
        up_out[planes + level : planes + level + 1, :] = top[planes + levels + level, SUB - 1 : SUB, :]
    up_out[planes + levels : planes + levels + 1, :] = top_depth
    down_out[0:planes, :] = bot_rows
    down_out[planes : planes + 1, :] = bot_d[0:1, :].astype(f32)
    for d in range(n_lon):
        for t in range(tiles):
            at = slice(t * LANES, (t + 1) * LANES)
            piece_out[d, t * planes : (t + 1) * planes, :] = top_rows[:, at]
            piece_out[d, lay.fold_depth + t : lay.fold_depth + t + 1, :] = top_depth[:, at]
        eastward = d == lax.rem(me + 1, n_lon)
        piece_out[d, lay.columns : lay.columns + 16, :] = jnp.where(eastward, east_rows, west_rows)
        piece_out[d, lay.owned : lay.owned + SUB, :] = own


def pack(lay, n_lon, owned, ocean, depth):
    rows, cols = ocean.shape[1:]
    full = pl.BlockSpec(memory_space=pltpu.VMEM)
    return pl.pallas_call(
        functools.partial(pack_kernel, lay),
        out_shape=(
            jax.ShapeDtypeStruct((n_lon, lay.size, LANES), f32),
            jax.ShapeDtypeStruct((lay.row_fields, cols), f32),
            jax.ShapeDtypeStruct((lay.row_fields, cols), f32),
        ),
        in_specs=[SMEM_SPEC, ANY, ANY],
        out_specs=(full, full, full),
        scratch_shapes=[
            pltpu.VMEM((4 * lay.levels, SUB, cols), f32),
            pltpu.VMEM((SUB, cols), jnp.int32),
            pltpu.VMEM((lay.planes, SUB, cols), f32),
            pltpu.VMEM((SUB, cols), jnp.int32),
            pltpu.VMEM((lay.planes, rows, LANES), f32),
            pltpu.VMEM((rows, LANES), jnp.int32),
            pltpu.VMEM((lay.planes + lay.levels, rows, LANES), f32),
            pltpu.VMEM((rows, LANES), jnp.int32),
            pltpu.VMEM((rows, LANES), f32),
            pltpu.SemaphoreType.DMA((8,)),
        ],
        name="pack",
    )(owned, ocean, depth)


def face(lower, upper, vel, shut_above, level):
    quarter = TIME_STEP * vel
    away = jnp.maximum(quarter, 0.0) + TIME_STEP * MIX_HORIZ
    back = quarter - away
    is_open = float(level) < shut_above
    zero = jnp.zeros((SUB, LANES), f32)
    away = jnp.where(is_open, away, zero)
    back = jnp.where(is_open, back, zero)
    return [away * a + back * b for a, b in zip(lower, upper, strict=True)]


def main_kernel(
    lay, n_lon, n_lat, slots,
    partner, ocean, depth, vert, got, from_south, from_north,
    vel, mass, strength, mask, vel_alias,
    out, ice_out,
    cbuf, ubuf, vbuf, mbuf, dint, dbuf, obuf, fold, sides, lists, hal_e, hal_w, gprev, ndep,
    fields, mask_v, depth_v, tile_sems, st, cf, in_sems, out_sems, list_sems, got_sems,
):
    planes, levels, tiles = lay.planes, lay.levels, lay.tiles
    rows, cols = depth.shape
    blocks = rows // SUB
    me, row_at = lax.axis_index("lon"), lax.axis_index("lat")
    tiles_dev = cols // TILE
    east_dev, west_dev = lax.rem(me + 1, n_lon), lax.rem(me + n_lon - 1, n_lon)

    list_copies = [
        pltpu.make_async_copy(
            got.at[lax.rem(me + slot, n_lon), pl.ds(lay.owned, SUB), :], lists.at[slot - 1], list_sems.at[slot - 1]
        )
        for slot in range(1, slots)
    ]
    for copy in list_copies:
        copy.start()
    start = partner[0]
    source = start // cols
    before = lax.rem(source + n_lon - 1, n_lon)
    got_copies = [
        pltpu.make_async_copy(got.at[source], fold.at[1], got_sems.at[0]),
        pltpu.make_async_copy(got.at[before], fold.at[0], got_sems.at[1]),
        pltpu.make_async_copy(got.at[east_dev, pl.ds(lay.columns, 16), :], sides.at[0], got_sems.at[2]),
        pltpu.make_async_copy(got.at[west_dev, pl.ds(lay.columns, 16), :], sides.at[1], got_sems.at[3]),
    ]
    in_copies = [
        pltpu.make_async_copy(depth, dint, in_sems.at[0]),
        pltpu.make_async_copy(ocean.at[0:planes], cbuf.at[:, 0:rows, :], in_sems.at[1]),
        pltpu.make_async_copy(ocean.at[planes : planes + levels], ubuf, in_sems.at[2]),
        pltpu.make_async_copy(ocean.at[planes + levels : planes + 2 * levels], vbuf, in_sems.at[3]),
        pltpu.make_async_copy(vert, mbuf, in_sems.at[4]),
    ]
    tile_refs = (vel, mass, strength, mask, depth, ocean)
    for copy in list_copies:
        copy.wait()
    listed, local = [], []
    for slot in range(1, slots):
        column = lists[slot - 1, 0, slot].astype(jnp.int32)
        listed.append(column >= 0)
        local.append(jnp.clip(column - me * tiles_dev, 0, tiles_dev - 1))
    for slot in range(1, slots):

        @pl.when(listed[slot - 1])
        def _():
            for copy in tile_copies(
                local[slot - 1], tile_refs, fields.at[slot - 1], mask_v.at[slot - 1], depth_v.at[slot - 1],
                tile_sems.at[slot - 1],
            ):
                copy.start()

    for copy in got_copies + in_copies:
        copy.start()

    def write_back(slot):
        cols_at = pl.ds(pl.multiple_of(local[slot - 1] * TILE, TILE), TILE)
        return pltpu.make_async_copy(
            fields.at[slot - 1, 0:2], ice_out.at[:, :, cols_at], tile_sems.at[slot - 1, 0]
        )

    for slot in range(1, slots):

        @pl.when(listed[slot - 1])
        def _():
            for copy in tile_copies(
                local[slot - 1], tile_refs, fields.at[slot - 1], mask_v.at[slot - 1], depth_v.at[slot - 1],
                tile_sems.at[slot - 1],
            ):
                copy.wait()
            ice_tile(fields.at[slot - 1], mask_v.at[slot - 1], depth_v.at[slot - 1], st, cf)
            write_back(slot).start()

    lane, sub = lane_ids(), sub_ids()
    lane0, lane_last = lane == 0, lane == LANES - 1
    sub0, sub_last = sub == 0, sub == SUB - 1

    for copy in got_copies:
        copy.wait()
    pad = jnp.zeros((LANES - 16, LANES), f32)
    hal_e[...] = jnp.transpose(jnp.concatenate([sides[0], pad], axis=0))
    hal_w[...] = jnp.transpose(jnp.concatenate([sides[1], pad], axis=0))

    for copy in in_copies:
        copy.wait()

    at_top = row_at == n_lat - 1
    offset = lax.rem(start, cols)
    chunk, shift = offset // LANES, lax.rem(offset, LANES)
    index = lax.rem(shift - lane + LANES, LANES)
    from_upper = lane <= shift

    def fold_tile(pos, t):
        which, tile = pos // tiles, lax.rem(pos, tiles)
        tracers = fold[which, pl.ds(pl.multiple_of(tile * planes, SUB), planes), :]
        deep = fold[which, pl.ds(lay.fold_depth + tile, 1), :]
        return tracers, jnp.broadcast_to(deep, (SUB, LANES))

    for t in range(tiles):
        at = slice(t * LANES, (t + 1) * LANES)
        high, high_d = fold_tile(tiles + chunk - t, t)
        low, low_d = fold_tile(tiles + chunk - t - 1, t)
        def pick(a, b):
            return jnp.where(
                from_upper, jnp.take_along_axis(a, index, axis=1), jnp.take_along_axis(b, index, axis=1)
            )
        north = jnp.where(at_top, pick(high, low), from_north[0:planes, at])
        north_d = jnp.where(at_top, pick(high_d, low_d), from_north[planes : planes + 1, at])
        for p in range(planes):
            cbuf[p, rows : rows + SUB, at] = jnp.broadcast_to(north[p : p + 1], (SUB, LANES))
        dbuf[rows : rows + SUB, at] = north_d
    for b in range(blocks):
        dbuf[b * SUB : (b + 1) * SUB, :] = dint[b * SUB : (b + 1) * SUB, :].astype(f32)

    def tracers_of(level):
        return (level, levels + level)

    not_bottom = row_at > 0
    for t in range(tiles):
        at = slice(t * LANES, (t + 1) * LANES)
        deep = jnp.where(not_bottom, from_south[planes + levels : planes + levels + 1, at], 0.0)
        shut = jnp.minimum(jnp.broadcast_to(deep, (SUB, LANES)), north_of(dbuf[0:SUB, at], dbuf[0:SUB, at], sub0))
        for level in range(levels):
            lower = [jnp.broadcast_to(from_south[p : p + 1, at], (SUB, LANES)) for p in tracers_of(level)]
            upper = [north_of(cbuf[p, 0:SUB, at], cbuf[p, 0:SUB, at], sub0) for p in tracers_of(level)]
            speed = jnp.broadcast_to(from_south[planes + level : planes + level + 1, at], (SUB, LANES))
            for p, g in zip(tracers_of(level), face(lower, upper, speed, shut, level), strict=True):
                gprev[p, :, at] = g

    zero = jnp.zeros((SUB, LANES), f32)

    def one_block(b, carry):
        r0 = pl.multiple_of(b * SUB, SUB)
        here, ahead = pl.ds(r0, SUB), pl.ds(pl.multiple_of(r0 + SUB, SUB), SUB)
        side_e, side_w = hal_e[here, :], hal_w[here, :]

        def load_c(t):
            at = slice(t * LANES, (t + 1) * LANES)
            return [cbuf[p, here, at] for p in range(planes)]

        cur, cur_d = load_c(0), dbuf[here, 0:LANES]
        shut = jnp.minimum(pltpu.roll(side_w, (LANES - 1 - (planes + levels)) % LANES, 1), pltpu.roll(cur_d, LANES - 1, 1))
        g_prev = [None] * planes
        for level in range(levels):
            lower = [pltpu.roll(side_w, LANES - 1 - p, 1) for p in tracers_of(level)]
            upper = [pltpu.roll(cur[p], LANES - 1, 1) for p in tracers_of(level)]
            speed = pltpu.roll(side_w, LANES - 1 - (planes + level), 1)
            for p, g in zip(tracers_of(level), face(lower, upper, speed, shut, level), strict=True):
                g_prev[p] = g
        for t in range(tiles):
            at = slice(t * LANES, (t + 1) * LANES)
            if t + 1 < tiles:
                nxt, nxt_d = load_c(t + 1), dbuf[here, (t + 1) * LANES : (t + 2) * LANES]
            else:
                nxt = [pltpu.roll(side_e, (LANES - p) % LANES, 1) for p in range(planes)]
                nxt_d = pltpu.roll(side_e, LANES - planes, 1)
            shut_e = jnp.minimum(cur_d, east_of(cur_d, nxt_d, lane0))
            shut_n = jnp.minimum(cur_d, north_of(cur_d, dbuf[ahead, at], sub0))
            interim = [None] * planes
            for level in range(levels):
                pair = tracers_of(level)
                lower = [cur[p] for p in pair]
                east = [east_of(cur[p], nxt[p], lane0) for p in pair]
                north = [north_of(cur[p], cbuf[p, ahead, at], sub0) for p in pair]
                g_east = face(lower, east, ubuf[level, here, at], shut_e, level)
                g_north = face(lower, north, vbuf[level, here, at], shut_n, level)
                for p, c, ge, gn in zip(pair, lower, g_east, g_north, strict=True):
                    g_west = west_of(ge, g_prev[p], lane_last)
                    g_south = south_of(gn, gprev[p, :, at], sub_last)
                    gprev[p, :, at] = gn
                    g_prev[p] = ge
                    interim[p] = c - ((ge - g_west) + (gn - g_south))
            mix = [
                jnp.where(float(level) < cur_d, TIME_STEP * mbuf[level, here, at], zero) for level in range(levels)
            ]
            ratio = [None] * levels
            solved = [None] * planes
            y = [[None] * levels, [None] * levels]
            for level in range(levels):
                diag = mix[level] + 1.0
                if level + 1 < levels:
                    diag = diag + mix[level + 1]
                if level:
                    ratio[level] = mix[level] * inv
                    diag = diag - mix[level] * ratio[level]
                inv = 1.0 / diag
                for tracer in range(2):
                    rhs = interim[tracer * levels + level]
                    if level:
                        rhs = rhs + mix[level] * y[tracer][level - 1]
                    y[tracer][level] = rhs * inv
            for tracer in range(2):
                z = y[tracer][levels - 1]
                obuf[tracer * levels + levels - 1, here, at] = z
                for level in range(levels - 2, -1, -1):
                    z = y[tracer][level] + ratio[level + 1] * z
                    obuf[tracer * levels + level, here, at] = z
            cur, cur_d = nxt, nxt_d
        return carry

    parts = out_sems.shape[0]
    per = blocks // parts

    def out_copy(part):
        at = pl.ds(part * per * SUB, per * SUB)
        return pltpu.make_async_copy(obuf.at[:, at, :], out.at[:, at, :], out_sems.at[part])

    for part in range(parts):
        lax.fori_loop(part * per, (part + 1) * per, one_block, 0)
        out_copy(part).start()
    for slot in range(1, slots):

        @pl.when(listed[slot - 1])
        def _():
            write_back(slot).wait()

    for part in range(parts):
        out_copy(part).wait()


def main(lay, n_lon, n_lat, slots, partner, ocean, depth, vert, got, south, north, vel, mass, strength, mask, ice):
    rows, cols = depth.shape
    levels, planes = lay.levels, lay.planes
    full = pl.BlockSpec(memory_space=pltpu.VMEM)
    extra = slots - 1
    return pl.pallas_call(
        functools.partial(main_kernel, lay, n_lon, n_lat, slots),
        out_shape=(
            jax.ShapeDtypeStruct((planes, rows, cols), f32),
            jax.ShapeDtypeStruct(ice.shape, f32),
        ),
        in_specs=[SMEM_SPEC, ANY, ANY, ANY, ANY, full, full] + [ANY] * 5,
        out_specs=(ANY, ANY),
        input_output_aliases={11: 1},
        scratch_shapes=[
            pltpu.VMEM((planes, rows + SUB, cols), f32),
            pltpu.VMEM((levels, rows, cols), f32),
            pltpu.VMEM((levels, rows, cols), f32),
            pltpu.VMEM((levels, rows, cols), f32),
            pltpu.VMEM((rows, cols), jnp.int32),
            pltpu.VMEM((rows + SUB, cols), f32),
            pltpu.VMEM((planes, rows, cols), f32),
            pltpu.VMEM((2, lay.size, LANES), f32),
            pltpu.VMEM((2, 16, LANES), f32),
            pltpu.SMEM((extra, SUB, LANES), f32),
            pltpu.VMEM((rows, LANES), f32),
            pltpu.VMEM((rows, LANES), f32),
            pltpu.VMEM((planes, SUB, cols), f32),
            pltpu.VMEM((SUB, LANES), f32),
            pltpu.VMEM((extra, 6, TILE, TILE), f32),
            pltpu.VMEM((extra, TILE, TILE), jnp.int32),
            pltpu.VMEM((extra, TILE, TILE), jnp.int32),
            pltpu.SemaphoreType.DMA((extra, TILE_COPIES)),
            pltpu.VMEM((5, N_VEC, SUB, LANES), f32),
            pltpu.VMEM((6, N_VEC, SUB, LANES), f32),
            pltpu.SemaphoreType.DMA((5,)),
            pltpu.SemaphoreType.DMA((4,)),
            pltpu.SemaphoreType.DMA((extra,)),
            pltpu.SemaphoreType.DMA((4,)),
        ],
        name="main",
    )(partner, ocean, depth, vert, got, south, north, vel, mass, strength, mask, ice)


def on_device(
    ocean_state,
    depth_levels,
    vert_mix,
    partner,
    ice_velocity,
    ice_mass,
    ice_strength,
    ice_mask,
    ice_owned,
):
    n_lon, n_lat = lax.axis_size("lon"), lax.axis_size("lat")
    fields, levels, rows, cols = ocean_state.shape
    ocean = ocean_state.reshape(fields * levels, rows, cols)
    lay = Layout(fields * levels, rows, cols)
    piece, up, down = pack(lay, n_lon, ice_owned, ocean, depth_levels)
    got = lax.all_to_all(piece, "lon", 0, 0, tiled=True)
    south = lax.ppermute(up, "lat", [(i, i + 1) for i in range(n_lat - 1)])
    north = lax.ppermute(down, "lat", [(i + 1, i) for i in range(n_lat - 1)])
    ice = first_ice(ice_owned, ice_velocity, ice_mass, ice_strength, ice_mask, depth_levels, ocean)
    tracers, ice = main(
        lay, n_lon, n_lat, ice_owned.shape[2], partner, ocean, depth_levels, vert_mix, got, south, north,
        ice_velocity, ice_mass, ice_strength, ice_mask, ice,
    )
    return tracers.reshape(2, levels, rows, cols), ice


def solution(mesh):
    return jax.shard_map(
        on_device,
        mesh=mesh,
        in_specs=(
            P(None, None, "lat", "lon"),
            P("lat", "lon"),
            P(None, "lat", "lon"),
            P("lon"),
            P(None, "lat", "lon"),
            P("lat", "lon"),
            P("lat", "lon"),
            P("lat", "lon"),
            P("lat", "lon", None),
        ),
        out_specs=(P(None, None, "lat", "lon"), P(None, "lat", "lon")),
        check_vma=False,
    )
```

profile of v0, /device:TPU:14, one launch (start us, length us, event | category | flops | bytes accessed | tf_op | source)
XLA Modules:
  0.0 52.7 jit_solution(16322237902322387247)
XLA Ops:
  0.6 3.4 %pack.1 = (f32[8,96,128]{2,1,0:T(8,128)}, f32[16,1024]{1,0:T(8,128)}, f32[16,1024]{1,0:T(8,128)}) custom-call(s32[1,1,3]{2,1,0:T(1,128)} %owned.3, f32[16,128,1024]{2,1,0:T(8,128)} %bitcast.2, s32[128,1024]{1,0:T(8,128)} %depth.5), custom_call_target="tpu_custom_call" | custom-call | tf_op jit(solution)/shard_map/pack/pallas_call | solution.py:321
  4.0 4.2 %all-to-all-start = ((f32[8,96,128]{2,1,0:T(8,128)}), f32[8,96,128]{2,1,0:T(8,128)S(1)}, u32[]{:S(2)}, u32[]{:S(2)}) async-start(f32[8,96,128]{2,1,0:T(8,128)} %get-tuple-element.7), calls=%async_computation | async-start | bytes 786432 | tf_op jit(solution)/shard_map/all_to_all | solution.py:642
  8.2 3.5 %collective-permute-start = (f32[16,1024]{1,0:T(8,128)}, f32[16,1024]{1,0:T(8,128)S(1)}, u32[]{:S(2)}, u32[]{:S(2)}) collective-permute-start(f32[16,1024]{1,0:T(8,128)} %get-tuple-element.8), channel_id=1, source_target_pairs={{0,1},{1,2},{2,3},{4,5},{5,6},{6,7},{8,9},{9,10},{10,11},{12,13},{... | collective-permute-start | bytes 196616 | tf_op jit(solution)/shard_map/ppermute | solution.py:643
  11.7 2.4 %collective-permute-start.1 = (f32[16,1024]{1,0:T(8,128)}, f32[16,1024]{1,0:T(8,128)S(1)}, u32[]{:S(2)}, u32[]{:S(2)}) collective-permute-start(f32[16,1024]{1,0:T(8,128)} %get-tuple-element.9), channel_id=1, source_target_pairs={{1,0},{2,1},{3,2},{5,4},{6,5},{7,6},{9,8},{10,9},{11,10},{13,12},{... | collective-permute-start | bytes 196616 | tf_op jit(solution)/shard_map/ppermute | solution.py:644
  14.1 10.5 %ice_first.1.vel_alias = f32[2,128,1024]{2,1,0:T(8,128)} custom-call(s32[1,1,3]{2,1,0:T(1,128)} %owned.3, f32[2,128,1024]{2,1,0:T(8,128)} %vel.3, f32[128,1024]{1,0:T(8,128)} %mass.3, f32[128,1024]{1,0:T(8,128)} %strength.3, s32[128,1024]{1,0:T(8,128)} %mask.3, s32[128,1024]{1,0:T(8,128)} %depth.5, f32[16,128,1024]{2,1,0:T(8,128)} %bitcast.3), custom_call_target="tpu_custom_call" | custom-call | tf_op jit(solution)/shard_map/ice_first/pallas_call | solution.py:229
  24.6 0.0 collective-permute-done.from_south
  24.6 0.0 copy-start.1
  24.6 0.0 collective-permute-done.1.from_north
  24.6 0.0 copy-start.2
  24.6 0.0 all-to-all-done.got
  24.7 0.6 %copy-done.1 = f32[16,1024]{1,0:T(8,128)} copy-done((f32[16,1024]{1,0:T(8,128)}, f32[16,1024]{1,0:T(8,128)S(1)}, u32[]{:S(2)}) %copy-start.1) | copy-done | bytes 65560
  25.3 0.0 copy-done.2
  25.3 0.0 copy-start
  25.3 0.7 %copy-done = f32[8,96,128]{2,1,0:T(8,128)} copy-done((f32[8,96,128]{2,1,0:T(8,128)}, f32[8,96,128]{2,1,0:T(8,128)S(1)}, u32[]{:S(2)}) %copy-start) | copy-done | bytes 393240
  26.0 26.7 %main.1 = (f32[8,128,1024]{2,1,0:T(8,128)}, f32[2,128,1024]{2,1,0:T(8,128)}) custom-call(s32[1024]{0:T(1024)} %partner.1, f32[16,128,1024]{2,1,0:T(8,128)} %bitcast.4, s32[128,1024]{1,0:T(8,128)} %depth.5, f32[4,128,1024]{2,1,0:T(8,128)} %vert.1, f32[8,96,128]{2,1,0:T(8,128)} %copy-done, f32[16,1024]{1,0:T(8,128)} %copy-done.1, ...), custom_call_target="tpu_custom_call", output_to_operand_aliasing={{1}: (11, {})} | custom-call | tf_op jit(solution)/shard_map/main/pallas_call | solution.py:587
Async XLA Ops:
  4.0 20.6 %all-to-all-start = ((f32[8,96,128]{2,1,0:T(8,128)}), f32[8,96,128]{2,1,0:T(8,128)S(1)}, u32[]{:S(2)}, u32[]{:S(2)}) async-start(f32[8,96,128]{2,1,0:T(8,128)} %get-tuple-element.7), calls=%async_computation | async-start | bytes 786432 | tf_op jit(solution)/shard_map/all_to_all | solution.py:642
  8.2 16.4 %collective-permute-start = (f32[16,1024]{1,0:T(8,128)}, f32[16,1024]{1,0:T(8,128)S(1)}, u32[]{:S(2)}, u32[]{:S(2)}) collective-permute-start(f32[16,1024]{1,0:T(8,128)} %get-tuple-element.8), channel_id=1, source_target_pairs={{0,1},{1,2},{2,3},{4,5},{5,6},{6,7},{8,9},{9,10},{10,11},{12,13},{... | collective-permute-start | bytes 196616 | tf_op jit(solution)/shard_map/ppermute | solution.py:643
  11.7 12.9 %collective-permute-start.1 = (f32[16,1024]{1,0:T(8,128)}, f32[16,1024]{1,0:T(8,128)S(1)}, u32[]{:S(2)}, u32[]{:S(2)}) collective-permute-start(f32[16,1024]{1,0:T(8,128)} %get-tuple-element.9), channel_id=1, source_target_pairs={{1,0},{2,1},{3,2},{5,4},{6,5},{7,6},{9,8},{10,9},{11,10},{13,12},{... | collective-permute-start | bytes 196616 | tf_op jit(solution)/shard_map/ppermute | solution.py:644
  24.6 0.6 %copy-start.1 = (f32[16,1024]{1,0:T(8,128)}, f32[16,1024]{1,0:T(8,128)S(1)}, u32[]{:S(2)}) copy-start(f32[16,1024]{1,0:T(8,128)S(1)} %collective-permute-done.from_south) | copy-start | bytes 196612
  24.6 0.6 %copy-start.2 = (f32[16,1024]{1,0:T(8,128)}, f32[16,1024]{1,0:T(8,128)S(1)}, u32[]{:S(2)}) copy-start(f32[16,1024]{1,0:T(8,128)S(1)} %collective-permute-done.1.from_north) | copy-start | bytes 196612
  25.3 0.7 %copy-start = (f32[8,96,128]{2,1,0:T(8,128)}, f32[8,96,128]{2,1,0:T(8,128)S(1)}, u32[]{:S(2)}) copy-start(f32[8,96,128]{2,1,0:T(8,128)S(1)} %all-to-all-done.got) | copy-start | bytes 1179652
where the time goes:
time: 53.2 us; the launch traced here: 52.7 us
  Pallas kernels  40.6 us (76%)
  starting transfers between devices  10 us (19%)
  local copies, waits for them, and re-layouts  1.35 us (3%)
  between operations  0.7 us (1%)
    pallas_call x1, Pallas kernels, main(): pl.pallas_call(functools.partial(main_kernel, lay, n_lon, n_lat, slots),...  26.7 us
    pallas_call x1, Pallas kernels, first_ice(): pl.pallas_call(first_ice_kernel, out_shape=jax.ShapeDtypeStruct(vel.shape...  10.5 us
    all_to_all x1, starting transfers between devices, on_device(): got = lax.all_to_all(piece, 'lon', 0, 0, tiled=True)  4.21 us
    ppermute x1, starting transfers between devices, on_device(): south = lax.ppermute(up, 'lat', [(i, i + 1) for i in range(n_lat - 1)])  3.47 us
    pallas_call x1, Pallas kernels, pack(): pl.pallas_call(functools.partial(pack_kernel, lay), out_shape=(jax.ShapeD...  3.38 us
    ppermute x1, starting transfers between devices, on_device(): north = lax.ppermute(down, 'lat', [(i + 1, i) for i in range(n_lat - 1)])  2.36 us
    unnamed x6, local copies, waits for them, and re-layouts  1.35 us
  transfers between devices with their start and end apart: 3, of which 0 were waited for; matrix products, arithmetic and copies ran while one was open for 0% of the time, Pallas kernels for 20%

commit v1 on v0

--- a/solution.py
+++ b/solution.py
@@ -11,6 +11,8 @@
 SUBCYCLES = 32
 LANES = 128
 SUB = 8
+MAIN_VMEM = 54_000_000
+FIRST_VMEM = 54_000_000
 
 TIME_STEP = 0.25
 MIX_HORIZ = 0.5
@@ -22,7 +24,7 @@
 CORIOLIS_PARAM = 0.5
 
 f32 = jnp.float32
-ANY = pl.BlockSpec(memory_space=pl.ANY)
+ANY = pl.BlockSpec(memory_space=pltpu.HBM)
 SMEM_SPEC = pl.BlockSpec(memory_space=pltpu.SMEM)
 
 
@@ -53,26 +55,12 @@
 N_VEC = TILE // SUB
 
 
-def ice_tile(fields, mask_ref, depth_ref, st, cf):
+def ice_prepare(fields, mask_ref, depth_ref, st, cf):
     lane, sub = lane_ids(), sub_ids()
-    lane_first, lane_last = lane == 0, lane == LANES - 1
-    sub_first, sub_last = sub == 0, sub == SUB - 1
     zero = jnp.zeros((SUB, LANES), f32)
 
     def rows(ref, index, v):
         return ref[index, pl.ds(v, SUB, stride=N_VEC), :]
-
-    def ahead_lane(x):
-        return jnp.where(lane_last, zero, pltpu.roll(x, LANES - 1, 1))
-
-    def behind_lane(x):
-        return jnp.where(lane_first, zero, pltpu.roll(x, 1, 1))
-
-    def ahead_wrap(x):
-        return jnp.where(sub_last, zero, pltpu.roll(x, SUB - 1, 0))
-
-    def behind_wrap(x):
-        return jnp.where(sub_first, zero, pltpu.roll(x, 1, 0))
 
     half_p = []
     for v in range(N_VEC):
@@ -92,61 +80,74 @@
         st[2, v] = half
         st[3, v] = half
         st[4, v] = zero
-        cf[0, v] = strength * (1.0 / 12.0)
+        cf[0, v] = strength * (2.0**0.5 / 12.0)
         cf[1, v] = inertia
         cf[2, v] = diag * inv
         cf[3, v] = turn * inv
     for v in range(N_VEC):
         half = half_p[v]
-        below = half_p[v - 1] if v else behind_wrap(half_p[N_VEC - 1])
-        cf[4, v] = WATER_DRAG * rows(fields, 4, v) - (half - behind_lane(half))
+        if v:
+            below = half_p[v - 1]
+        else:
+            below = jnp.where(sub == 0, zero, pltpu.roll(half_p[N_VEC - 1], 1, 0))
+        west = jnp.where(lane == 0, zero, pltpu.roll(half, 1, 1))
+        cf[4, v] = WATER_DRAG * rows(fields, 4, v) - (half - west)
         cf[5, v] = WATER_DRAG * rows(fields, 5, v) - (half - below)
 
+
+def ice_cycles(tiles, cycles):
+    lane, sub = lane_ids(), sub_ids()
+    lane_first, lane_last = lane == 0, lane == LANES - 1
+    sub_first, sub_last = sub == 0, sub == SUB - 1
+    zero = jnp.zeros((SUB, LANES), f32)
     keep = 1.0 / (1.0 + RELAX_RATE)
 
+    def ahead_lane(x):
+        return jnp.where(lane_last, zero, pltpu.roll(x, LANES - 1, 1))
+
+    def behind_lane(x):
+        return jnp.where(lane_first, zero, pltpu.roll(x, 1, 1))
+
+    def ahead_row(st, i, v):
+        if v + 1 < N_VEC:
+            return st[i, v + 1]
+        return jnp.where(sub_last, zero, pltpu.roll(st[i, 0], SUB - 1, 0))
+
+    def behind_row(st, i, v):
+        if v:
+            return st[i, v - 1]
+        return jnp.where(sub_first, zero, pltpu.roll(st[i, N_VEC - 1], 1, 0))
+
     def one_cycle(_, carry):
-        def update(v, u, w, sxx, syy, s12, syy_below, s12_below):
-            fx = (sxx - behind_lane(sxx)) + (s12 - s12_below)
-            fy = (s12 - behind_lane(s12)) + (syy - syy_below)
-            inertia, ca, cb = cf[1, v], cf[2, v], cf[3, v]
-            rx = inertia * u + (fx + cf[4, v])
-            ry = inertia * w + (fy + cf[5, v])
-            st[0, v] = ca * rx + cb * ry
-            st[1, v] = ca * ry - cb * rx
-
-        u, w = st[0, 0], st[1, 0]
-        first_u, first_w = u, w
-        first = prev = None
-        for v in range(N_VEC):
-            if v + 1 < N_VEC:
-                u_north, w_north = st[0, v + 1], st[1, v + 1]
-            else:
-                u_north, w_north = ahead_wrap(first_u), ahead_wrap(first_w)
-            ux = ahead_lane(u) - u
-            vy = w_north - w
-            shear = (u_north - u) + (ahead_lane(w) - w)
-            div = ux + vy
-            tens = ux - vy
-            div2 = div + div
-            four = div2 * div2 + (tens * tens + (shear * shear + 4.0 * DELTA_FLOOR_SQ))
-            k = cf[0, v] * lax.rsqrt(four)
-            div4 = div2 + div2
-            sxx = keep * st[2, v] + k * (div4 + tens)
-            syy = keep * st[3, v] + k * (div4 - tens)
-            s12 = keep * st[4, v] + (k + k) * shear
-            st[2, v] = sxx
-            st[3, v] = syy
-            st[4, v] = s12
-            if v == 0:
-                first = (sxx, syy, s12)
-            else:
-                update(v, u, w, sxx, syy, s12, prev[1], prev[2])
-            prev = (sxx, syy, s12)
-            u, w = u_north, w_north
-        update(0, first_u, first_w, *first, behind_wrap(prev[1]), behind_wrap(prev[2]))
+        for st, cf in tiles:
+            for v in range(N_VEC):
+                u, w = st[0, v], st[1, v]
+                ux = ahead_lane(u) - u
+                vy = ahead_row(st, 1, v) - w
+                shear = (ahead_row(st, 0, v) - u) + (ahead_lane(w) - w)
+                both = 1.5 * (ux + vy)
+                xx, yy = both + ux, both + vy
+                two = (ux * xx + vy * yy) + ((0.5 * shear) * shear + 2.0 * DELTA_FLOOR_SQ)
+                k = cf[0, v] * lax.rsqrt(two)
+                st[2, v] = keep * st[2, v] + k * xx
+                st[3, v] = keep * st[3, v] + k * yy
+                st[4, v] = keep * st[4, v] + k * shear
+            for v in range(N_VEC):
+                u, w = st[0, v], st[1, v]
+                sxx, syy, s12 = st[2, v], st[3, v], st[4, v]
+                fx = (sxx - behind_lane(sxx)) + (s12 - behind_row(st, 4, v))
+                fy = (s12 - behind_lane(s12)) + (syy - behind_row(st, 3, v))
+                inertia, ca, cb = cf[1, v], cf[2, v], cf[3, v]
+                rx = inertia * u + (fx + cf[4, v])
+                ry = inertia * w + (fy + cf[5, v])
+                st[0, v] = ca * rx + cb * ry
+                st[1, v] = ca * ry - cb * rx
         return carry
 
-    lax.fori_loop(0, SUBCYCLES, one_cycle, 0)
+    lax.fori_loop(0, cycles, one_cycle, 0)
+
+
+def ice_finish(st, fields):
     for v in range(N_VEC):
         fields[0, pl.ds(v, SUB, stride=N_VEC), :] = st[0, v]
         fields[1, pl.ds(v, SUB, stride=N_VEC), :] = st[1, v]
@@ -168,77 +169,42 @@
 
 
 TILE_COPIES = 7
-
-
-def ice_scratch():
-    return [
-        pltpu.VMEM((6, TILE, TILE), f32),
-        pltpu.VMEM((TILE, TILE), jnp.int32),
-        pltpu.VMEM((TILE, TILE), jnp.int32),
-        pltpu.SemaphoreType.DMA((TILE_COPIES,)),
-    ]
+FIRST_CYCLES = 14
+ST_SHAPE, CF_SHAPE = (5, N_VEC, SUB, LANES), (6, N_VEC, SUB, LANES)
 
 
 def first_ice_kernel(
-    owned, vel, mass, strength, mask, depth, ocean, out,
-    fields, mask_v, depth_v, sems, st, cf, all_vel, copy_sems, all_sem,
+    owned, vel, mass, strength, mask, depth, ocean, st, cf, fields, mask_v, depth_v, sems
 ):
     tiles_dev = vel.shape[2] // TILE
     column = owned[0, 0, 0]
-    listed = column >= 0
-    local = jnp.where(listed, column - lax.axis_index("lon") * tiles_dev, -1)
-    safe = jnp.clip(local, 0, tiles_dev - 1)
-    refs = (vel, mass, strength, mask, depth, ocean)
-    whole = pltpu.make_async_copy(vel, all_vel, all_sem)
-
-    def pass_through(q):
-        cols = pl.ds(q * TILE, TILE)
-        return pltpu.make_async_copy(all_vel.at[:, :, cols], out.at[:, :, cols], copy_sems.at[q])
-
-    @pl.when(listed)
+    local = jnp.clip(column - lax.axis_index("lon") * tiles_dev, 0, tiles_dev - 1)
+
+    @pl.when(column >= 0)
     def _():
-        for copy in tile_copies(safe, refs, fields, mask_v, depth_v, sems):
+        copies = tile_copies(local, (vel, mass, strength, mask, depth, ocean), fields, mask_v, depth_v, sems)
+        for copy in copies:
             copy.start()
-
-    whole.start()
-    whole.wait()
-    for q in range(tiles_dev):
-
-        @pl.when(local != q)
-        def _():
-            pass_through(q).start()
-
-    @pl.when(listed)
-    def _():
-        for copy in tile_copies(safe, refs, fields, mask_v, depth_v, sems):
+        for copy in copies:
             copy.wait()
-        ice_tile(fields, mask_v, depth_v, st, cf)
-        cols = pl.ds(pl.multiple_of(safe * TILE, TILE), TILE)
-        back = pltpu.make_async_copy(fields.at[0:2], out.at[:, :, cols], sems.at[0])
-        back.start()
-        back.wait()
-
-    for q in range(tiles_dev):
-
-        @pl.when(local != q)
-        def _():
-            pass_through(q).wait()
+        ice_prepare(fields, mask_v, depth_v, st, cf)
+        ice_cycles([(st, cf)], FIRST_CYCLES)
 
 
 def first_ice(owned, vel, mass, strength, mask, depth, ocean):
+    full = pl.BlockSpec(memory_space=pltpu.VMEM)
     return pl.pallas_call(
         first_ice_kernel,
-        out_shape=jax.ShapeDtypeStruct(vel.shape, f32),
+        out_shape=(jax.ShapeDtypeStruct(ST_SHAPE, f32), jax.ShapeDtypeStruct(CF_SHAPE, f32)),
         in_specs=[SMEM_SPEC] + [ANY] * 6,
-        out_specs=ANY,
-        scratch_shapes=ice_scratch()
-        + [
-            pltpu.VMEM((5, N_VEC, SUB, LANES), f32),
-            pltpu.VMEM((6, N_VEC, SUB, LANES), f32),
-            pltpu.VMEM(vel.shape, f32),
-            pltpu.SemaphoreType.DMA((vel.shape[2] // TILE,)),
-            pltpu.SemaphoreType.DMA,
+        out_specs=(full, full),
+        scratch_shapes=[
+            pltpu.VMEM((6, TILE, TILE), f32),
+            pltpu.VMEM((TILE, TILE), jnp.int32),
+            pltpu.VMEM((TILE, TILE), jnp.int32),
+            pltpu.SemaphoreType.DMA((TILE_COPIES,)),
         ],
+        compiler_params=pltpu.CompilerParams(vmem_limit_bytes=FIRST_VMEM),
         name="ice_first",
     )(owned, vel, mass, strength, mask, depth, ocean)
 
@@ -343,6 +309,9 @@
     )(owned, ocean, depth)
 
 
+PART_BLOCKS = 2
+
+
 def face(lower, upper, vel, shut_above, level):
     quarter = TIME_STEP * vel
     away = jnp.maximum(quarter, 0.0) + TIME_STEP * MIX_HORIZ
@@ -356,11 +325,11 @@
 
 def main_kernel(
     lay, n_lon, n_lat, slots,
-    partner, ocean, depth, vert, got, from_south, from_north,
-    vel, mass, strength, mask, vel_alias,
+    partner, owned, ocean, depth, vert, got, from_south, from_north,
+    vel, mass, strength, mask, first_st, first_cf,
     out, ice_out,
-    cbuf, ubuf, vbuf, mbuf, dint, dbuf, obuf, fold, sides, lists, hal_e, hal_w, gprev, ndep,
-    fields, mask_v, depth_v, tile_sems, st, cf, in_sems, out_sems, list_sems, got_sems,
+    cbuf, ubuf, vbuf, mbuf, dint, dbuf, obuf, lists, hal_e, hal_w, gprev,
+    all_vel, fields, mask_v, depth_v, tile_sems, st, cf, first_sems, in_sems, out_sems, list_sems, pass_sems,
 ):
     planes, levels, tiles = lay.planes, lay.levels, lay.tiles
     rows, cols = depth.shape
@@ -380,70 +349,93 @@
     start = partner[0]
     source = start // cols
     before = lax.rem(source + n_lon - 1, n_lon)
-    got_copies = [
-        pltpu.make_async_copy(got.at[source], fold.at[1], got_sems.at[0]),
-        pltpu.make_async_copy(got.at[before], fold.at[0], got_sems.at[1]),
-        pltpu.make_async_copy(got.at[east_dev, pl.ds(lay.columns, 16), :], sides.at[0], got_sems.at[2]),
-        pltpu.make_async_copy(got.at[west_dev, pl.ds(lay.columns, 16), :], sides.at[1], got_sems.at[3]),
-    ]
     in_copies = [
         pltpu.make_async_copy(depth, dint, in_sems.at[0]),
         pltpu.make_async_copy(ocean.at[0:planes], cbuf.at[:, 0:rows, :], in_sems.at[1]),
         pltpu.make_async_copy(ocean.at[planes : planes + levels], ubuf, in_sems.at[2]),
         pltpu.make_async_copy(ocean.at[planes + levels : planes + 2 * levels], vbuf, in_sems.at[3]),
         pltpu.make_async_copy(vert, mbuf, in_sems.at[4]),
+        pltpu.make_async_copy(vel, all_vel, in_sems.at[5]),
     ]
     tile_refs = (vel, mass, strength, mask, depth, ocean)
     for copy in list_copies:
         copy.wait()
-    listed, local = [], []
+    columns = [owned[0, 0, 0]] + [lists[slot - 1, 0, slot].astype(jnp.int32) for slot in range(1, slots)]
+    listed = [column >= 0 for column in columns]
+    local = [jnp.clip(column - me * tiles_dev, 0, tiles_dev - 1) for column in columns]
+
+    def fields_in(slot):
+        i = slot - 1
+        return tile_copies(local[slot], tile_refs, fields.at[slot], mask_v.at[i], depth_v.at[i], tile_sems.at[slot])
+
+    first_copies = [
+        pltpu.make_async_copy(first_st, st.at[0], first_sems.at[0]),
+        pltpu.make_async_copy(first_cf, cf.at[0], first_sems.at[1]),
+    ]
+    for copy in first_copies:
+        copy.start()
     for slot in range(1, slots):
-        column = lists[slot - 1, 0, slot].astype(jnp.int32)
-        listed.append(column >= 0)
-        local.append(jnp.clip(column - me * tiles_dev, 0, tiles_dev - 1))
+
+        @pl.when(listed[slot])
+        def _():
+            for copy in fields_in(slot):
+                copy.start()
+
+    for copy in in_copies:
+        copy.start()
     for slot in range(1, slots):
 
-        @pl.when(listed[slot - 1])
+        @pl.when(listed[slot])
         def _():
-            for copy in tile_copies(
-                local[slot - 1], tile_refs, fields.at[slot - 1], mask_v.at[slot - 1], depth_v.at[slot - 1],
-                tile_sems.at[slot - 1],
-            ):
-                copy.start()
-
-    for copy in got_copies + in_copies:
-        copy.start()
+            for copy in fields_in(slot):
+                copy.wait()
+            ice_prepare(fields.at[slot], mask_v.at[slot - 1], depth_v.at[slot - 1], st.at[slot], cf.at[slot])
+
+    for copy in first_copies:
+        copy.wait()
+    some = functools.reduce(jnp.logical_or, listed)
+
+    @pl.when(some)
+    def _():
+        every = [(st.at[slot], cf.at[slot]) for slot in range(slots)]
+        ice_cycles(every, SUBCYCLES - FIRST_CYCLES)
+        ice_cycles(every[1:], FIRST_CYCLES)
 
     def write_back(slot):
-        cols_at = pl.ds(pl.multiple_of(local[slot - 1] * TILE, TILE), TILE)
-        return pltpu.make_async_copy(
-            fields.at[slot - 1, 0:2], ice_out.at[:, :, cols_at], tile_sems.at[slot - 1, 0]
+        at = pl.ds(pl.multiple_of(local[slot] * TILE, TILE), TILE)
+        return pltpu.make_async_copy(fields.at[slot, 0:2], ice_out.at[:, :, at], tile_sems.at[slot, 0])
+
+    def pass_through(q):
+        at = pl.ds(q * TILE, TILE)
+        return pltpu.make_async_copy(all_vel.at[:, :, at], ice_out.at[:, :, at], pass_sems.at[q])
+
+    def untouched(q):
+        return jnp.logical_not(
+            functools.reduce(jnp.logical_or, [on & (at == q) for on, at in zip(listed, local, strict=True)])
         )
 
-    for slot in range(1, slots):
-
-        @pl.when(listed[slot - 1])
+    for slot in range(slots):
+
+        @pl.when(listed[slot])
         def _():
-            for copy in tile_copies(
-                local[slot - 1], tile_refs, fields.at[slot - 1], mask_v.at[slot - 1], depth_v.at[slot - 1],
-                tile_sems.at[slot - 1],
-            ):
-                copy.wait()
-            ice_tile(fields.at[slot - 1], mask_v.at[slot - 1], depth_v.at[slot - 1], st, cf)
+            ice_finish(st.at[slot], fields.at[slot])
             write_back(slot).start()
 
     lane, sub = lane_ids(), sub_ids()
     lane0, lane_last = lane == 0, lane == LANES - 1
     sub0, sub_last = sub == 0, sub == SUB - 1
 
-    for copy in got_copies:
-        copy.wait()
     pad = jnp.zeros((LANES - 16, LANES), f32)
-    hal_e[...] = jnp.transpose(jnp.concatenate([sides[0], pad], axis=0))
-    hal_w[...] = jnp.transpose(jnp.concatenate([sides[1], pad], axis=0))
+    hal_e[...] = jnp.transpose(jnp.concatenate([got[east_dev, lay.columns : lay.columns + 16, :], pad], axis=0))
+    hal_w[...] = jnp.transpose(jnp.concatenate([got[west_dev, lay.columns : lay.columns + 16, :], pad], axis=0))
 
     for copy in in_copies:
         copy.wait()
+    for q in range(tiles_dev):
+
+        @pl.when(untouched(q))
+        def _():
+            pass_through(q).start()
 
     at_top = row_at == n_lat - 1
     offset = lax.rem(start, cols)
@@ -451,16 +443,16 @@
     index = lax.rem(shift - lane + LANES, LANES)
     from_upper = lane <= shift
 
-    def fold_tile(pos, t):
-        which, tile = pos // tiles, lax.rem(pos, tiles)
-        tracers = fold[which, pl.ds(pl.multiple_of(tile * planes, SUB), planes), :]
-        deep = fold[which, pl.ds(lay.fold_depth + tile, 1), :]
+    def fold_tile(pos):
+        which, tile = jnp.where(pos >= tiles, source, before), lax.rem(pos, tiles)
+        tracers = got[which, pl.ds(pl.multiple_of(tile * planes, SUB), planes), :]
+        deep = got[which, pl.ds(lay.fold_depth + tile, 1), :]
         return tracers, jnp.broadcast_to(deep, (SUB, LANES))
 
     for t in range(tiles):
         at = slice(t * LANES, (t + 1) * LANES)
-        high, high_d = fold_tile(tiles + chunk - t, t)
-        low, low_d = fold_tile(tiles + chunk - t - 1, t)
+        high, high_d = fold_tile(tiles + chunk - t)
+        low, low_d = fold_tile(tiles + chunk - t - 1)
         def pick(a, b):
             return jnp.where(
                 from_upper, jnp.take_along_axis(a, index, axis=1), jnp.take_along_axis(b, index, axis=1)
@@ -563,36 +555,44 @@
     per = blocks // parts
 
     def out_copy(part):
-        at = pl.ds(part * per * SUB, per * SUB)
+        at = pl.ds(pl.multiple_of(part * per * SUB, per * SUB), per * SUB)
         return pltpu.make_async_copy(obuf.at[:, at, :], out.at[:, at, :], out_sems.at[part])
 
-    for part in range(parts):
+    def one_part(part, carry):
         lax.fori_loop(part * per, (part + 1) * per, one_block, 0)
         out_copy(part).start()
-    for slot in range(1, slots):
-
-        @pl.when(listed[slot - 1])
+        return carry
+
+    lax.fori_loop(0, parts, one_part, 0)
+    for slot in range(slots):
+
+        @pl.when(listed[slot])
         def _():
             write_back(slot).wait()
 
+    for q in range(tiles_dev):
+
+        @pl.when(untouched(q))
+        def _():
+            pass_through(q).wait()
+
     for part in range(parts):
         out_copy(part).wait()
 
 
-def main(lay, n_lon, n_lat, slots, partner, ocean, depth, vert, got, south, north, vel, mass, strength, mask, ice):
+def main(lay, n_lon, n_lat, partner, owned, ocean, depth, vert, got, south, north, vel, mass, strength, mask, first):
     rows, cols = depth.shape
     levels, planes = lay.levels, lay.planes
+    slots = owned.shape[2]
     full = pl.BlockSpec(memory_space=pltpu.VMEM)
-    extra = slots - 1
     return pl.pallas_call(
         functools.partial(main_kernel, lay, n_lon, n_lat, slots),
         out_shape=(
             jax.ShapeDtypeStruct((planes, rows, cols), f32),
-            jax.ShapeDtypeStruct(ice.shape, f32),
+            jax.ShapeDtypeStruct(vel.shape, f32),
         ),
-        in_specs=[SMEM_SPEC, ANY, ANY, ANY, ANY, full, full] + [ANY] * 5,
+        in_specs=[SMEM_SPEC, SMEM_SPEC] + [ANY] * 3 + [full] * 3 + [ANY] * 6,
         out_specs=(ANY, ANY),
-        input_output_aliases={11: 1},
         scratch_shapes=[
             pltpu.VMEM((planes, rows + SUB, cols), f32),
             pltpu.VMEM((levels, rows, cols), f32),
@@ -601,26 +601,26 @@
             pltpu.VMEM((rows, cols), jnp.int32),
             pltpu.VMEM((rows + SUB, cols), f32),
             pltpu.VMEM((planes, rows, cols), f32),
-            pltpu.VMEM((2, lay.size, LANES), f32),
-            pltpu.VMEM((2, 16, LANES), f32),
-            pltpu.SMEM((extra, SUB, LANES), f32),
+            pltpu.SMEM((slots - 1, SUB, LANES), f32),
             pltpu.VMEM((rows, LANES), f32),
             pltpu.VMEM((rows, LANES), f32),
             pltpu.VMEM((planes, SUB, cols), f32),
-            pltpu.VMEM((SUB, LANES), f32),
-            pltpu.VMEM((extra, 6, TILE, TILE), f32),
-            pltpu.VMEM((extra, TILE, TILE), jnp.int32),
-            pltpu.VMEM((extra, TILE, TILE), jnp.int32),
-            pltpu.SemaphoreType.DMA((extra, TILE_COPIES)),
-            pltpu.VMEM((5, N_VEC, SUB, LANES), f32),
-            pltpu.VMEM((6, N_VEC, SUB, LANES), f32),
-            pltpu.SemaphoreType.DMA((5,)),
-            pltpu.SemaphoreType.DMA((4,)),
-            pltpu.SemaphoreType.DMA((extra,)),
-            pltpu.SemaphoreType.DMA((4,)),
+            pltpu.VMEM(vel.shape, f32),
+            pltpu.VMEM((slots, 6, TILE, TILE), f32),
+            pltpu.VMEM((slots - 1, TILE, TILE), jnp.int32),
+            pltpu.VMEM((slots - 1, TILE, TILE), jnp.int32),
+            pltpu.SemaphoreType.DMA((slots, TILE_COPIES)),
+            pltpu.VMEM((slots, *ST_SHAPE), f32),
+            pltpu.VMEM((slots, *CF_SHAPE), f32),
+            pltpu.SemaphoreType.DMA((2,)),
+            pltpu.SemaphoreType.DMA((6,)),
+            pltpu.SemaphoreType.DMA((rows // (PART_BLOCKS * SUB),)),
+            pltpu.SemaphoreType.DMA((slots - 1,)),
+            pltpu.SemaphoreType.DMA((cols // TILE,)),
         ],
+        compiler_params=pltpu.CompilerParams(vmem_limit_bytes=MAIN_VMEM),
         name="main",
-    )(partner, ocean, depth, vert, got, south, north, vel, mass, strength, mask, ice)
+    )(partner, owned, ocean, depth, vert, got, south, north, vel, mass, strength, mask, *first)
 
 
 def on_device(
@@ -642,10 +642,10 @@
     got = lax.all_to_all(piece, "lon", 0, 0, tiled=True)
     south = lax.ppermute(up, "lat", [(i, i + 1) for i in range(n_lat - 1)])
     north = lax.ppermute(down, "lat", [(i + 1, i) for i in range(n_lat - 1)])
-    ice = first_ice(ice_owned, ice_velocity, ice_mass, ice_strength, ice_mask, depth_levels, ocean)
+    first = first_ice(ice_owned, ice_velocity, ice_mass, ice_strength, ice_mask, depth_levels, ocean)
     tracers, ice = main(
-        lay, n_lon, n_lat, ice_owned.shape[2], partner, ocean, depth_levels, vert_mix, got, south, north,
-        ice_velocity, ice_mass, ice_strength, ice_mask, ice,
+        lay, n_lon, n_lat, partner, ice_owned, ocean, depth_levels, vert_mix, got, south, north,
+        ice_velocity, ice_mass, ice_strength, ice_mask, first,
     )
     return tracers.reshape(2, levels, rows, cols), ice
 

time: 53.2 us -> 42.8 us (0.80)
  Pallas kernels: 40.6 us -> 31.5 us
  local copies, waits for them, and re-layouts: 1.35 us -> 0.03 us
    pallas_call x1, Pallas kernels: 10.5 us -> 4.98 us  [first_ice(): pl.pallas_call(first_ice_kernel, out_shape=(jax.ShapeDtypeStruct(ST_SHAPE...]
    pallas_call x1, Pallas kernels: 26.7 us -> 23 us  [main(): pl.pallas_call(functools.partial(main_kernel, lay, n_lon, n_lat, slots),...]
    unnamed x6 -> x12, local copies, waits for them, and re-layouts: 1.35 us -> 0.03 us
  transfers between devices with their start and end apart: 3 -> 3, of which waited for: 0 -> 0; matrix products, arithmetic and copies ran while one was open for 0% -> 0% of each run, Pallas kernels for 20% -> 12%
where the time goes in v1:
time: 42.8 us; the launch traced here: 42.5 us
  Pallas kernels  31.5 us (74%)
  starting transfers between devices  10.2 us (24%)
  between operations  0.78 us (2%)
    pallas_call x1, Pallas kernels, main(): pl.pallas_call(functools.partial(main_kernel, lay, n_lon, n_lat, slots),...  23 us
    pallas_call x1, Pallas kernels, first_ice(): pl.pallas_call(first_ice_kernel, out_shape=(jax.ShapeDtypeStruct(ST_SHAPE...  4.98 us
    all_to_all x1, starting transfers between devices, on_device(): got = lax.all_to_all(piece, 'lon', 0, 0, tiled=True)  4.21 us
    pallas_call x1, Pallas kernels, pack(): pl.pallas_call(functools.partial(pack_kernel, lay), out_shape=(jax.ShapeD...  3.51 us
    ppermute x1, starting transfers between devices, on_device(): south = lax.ppermute(up, 'lat', [(i, i + 1) for i in range(n_lat - 1)])  3.47 us
    ppermute x1, starting transfers between devices, on_device(): north = lax.ppermute(down, 'lat', [(i + 1, i) for i in range(n_lat - 1)])  2.49 us
  transfers between devices with their start and end apart: 3, of which 0 were waited for; matrix products, arithmetic and copies ran while one was open for 0% of the time, Pallas kernels for 12%

profile of v1, /device:TPU:14, one launch (start us, length us, event | category | flops | bytes accessed | tf_op | source)
XLA Modules:
  0.0 42.5 jit_solution(5368862242272975791)
XLA Ops:
  0.6 0.0 copy-start.1
  0.6 0.0 copy-start.2
  0.7 0.0 copy-start.3
  0.7 0.0 copy-start.4
  0.7 3.5 %pack.1 = (f32[8,96,128]{2,1,0:T(8,128)}, f32[16,1024]{1,0:T(8,128)}, f32[16,1024]{1,0:T(8,128)}) custom-call(s32[1,1,3]{2,1,0:T(1,128)} %owned.5, f32[16,128,1024]{2,1,0:T(8,128)} %bitcast.2, s32[128,1024]{1,0:T(8,128)} %depth.5), custom_call_target="tpu_custom_call" | custom-call | tf_op jit(solution)/shard_map/pack/pallas_call | solution.py:287
  4.2 4.2 %all-to-all-start = ((f32[8,96,128]{2,1,0:T(8,128)}), f32[8,96,128]{2,1,0:T(8,128)S(1)}, u32[]{:S(2)}, u32[]{:S(2)}) async-start(f32[8,96,128]{2,1,0:T(8,128)} %get-tuple-element.9), calls=%async_computation | async-start | bytes 786432 | tf_op jit(solution)/shard_map/all_to_all | solution.py:642
  8.4 3.5 %collective-permute-start = (f32[16,1024]{1,0:T(8,128)}, f32[16,1024]{1,0:T(8,128)S(1)}, u32[]{:S(2)}, u32[]{:S(2)}) collective-permute-start(f32[16,1024]{1,0:T(8,128)} %get-tuple-element.10), channel_id=1, source_target_pairs={{0,1},{1,2},{2,3},{4,5},{5,6},{6,7},{8,9},{9,10},{10,11},{12,13},{... | collective-permute-start | bytes 196616 | tf_op jit(solution)/shard_map/ppermute | solution.py:643
  11.9 0.0 copy-start
  11.9 0.0 copy-start.5
  11.9 2.5 %collective-permute-start.1 = (f32[16,1024]{1,0:T(8,128)}, f32[16,1024]{1,0:T(8,128)S(1)}, u32[]{:S(2)}, u32[]{:S(2)}) collective-permute-start(f32[16,1024]{1,0:T(8,128)} %get-tuple-element.11), channel_id=1, source_target_pairs={{1,0},{2,1},{3,2},{5,4},{6,5},{7,6},{9,8},{10,9},{11,10},{13,12},{... | collective-permute-start | bytes 196616 | tf_op jit(solution)/shard_map/ppermute | solution.py:644
  14.4 0.0 copy-done.1
  14.4 0.0 copy-done.2
  14.4 0.0 copy-done.3
  14.4 0.0 copy-done.4
  14.4 5.0 %ice_first.1 = (f32[5,16,8,128]{3,2,1,0:T(8,128)S(1)}, f32[6,16,8,128]{3,2,1,0:T(8,128)S(1)}) custom-call(s32[1,1,3]{2,1,0:T(1,128)S(1)} %copy-done.4, f32[2,128,1024]{2,1,0:T(8,128)} %vel.3, f32[128,1024]{1,0:T(8,128)S(1)} %copy-done.1, f32[128,1024]{1,0:T(8,128)S(1)} %copy-done.2, s32[128,1024]{1,0:T(8,128)S(1)} %copy-done.3, s32[128,1024]{1,0:T(8,128)} %depth.5, ...), custom_call_target="tpu_custom_call" | custom-call | tf_op jit(solution)/shard_map/ice_first/pallas_call | solution.py:196
  19.4 0.0 collective-permute-done.from_south
  19.4 0.0 collective-permute-done.1.from_north
  19.4 0.0 all-to-all-done.got
  19.5 0.0 copy-done
  19.5 0.0 copy-done.5
  19.5 23.0 %main.1 = (f32[8,128,1024]{2,1,0:T(8,128)}, f32[2,128,1024]{2,1,0:T(8,128)}) custom-call(s32[1024]{0:T(1024)S(1)} %copy-done.5, s32[1,1,3]{2,1,0:T(1,128)S(1)} %copy-done.4, f32[16,128,1024]{2,1,0:T(8,128)} %bitcast.4, s32[128,1024]{1,0:T(8,128)S(1)} %copy-done, f32[4,128,1024]{2,1,0:T(8,128)} %vert.1, f32[8,96,128]{2,1,0:T(8,128)S(1)} %all-to-all-done.got, ...), custom_call_target="tpu_custom_call" | custom-call | tf_op jit(solution)/shard_map/main/pallas_call | solution.py:588
Async XLA Ops:
  0.6 13.8 %copy-start.1 = (f32[128,1024]{1,0:T(8,128)S(1)}, f32[128,1024]{1,0:T(8,128)}, u32[]{:S(2)}) copy-start(f32[128,1024]{1,0:T(8,128)} %mass.3) | copy-start | bytes 1572868
  0.6 13.8 %copy-start.2 = (f32[128,1024]{1,0:T(8,128)S(1)}, f32[128,1024]{1,0:T(8,128)}, u32[]{:S(2)}) copy-start(f32[128,1024]{1,0:T(8,128)} %strength.3) | copy-start | bytes 1572868
  0.7 13.8 %copy-start.3 = (s32[128,1024]{1,0:T(8,128)S(1)}, s32[128,1024]{1,0:T(8,128)}, u32[]{:S(2)}) copy-start(s32[128,1024]{1,0:T(8,128)} %mask.3) | copy-start | bytes 1572868
  0.7 13.8 %copy-start.4 = (s32[1,1,3]{2,1,0:T(1,128)S(1)}, s32[1,1,3]{2,1,0:T(1,128)}, u32[]{:S(2)}) copy-start(s32[1,1,3]{2,1,0:T(1,128)} %owned.5) | copy-start | bytes 40
  4.2 15.3 %all-to-all-start = ((f32[8,96,128]{2,1,0:T(8,128)}), f32[8,96,128]{2,1,0:T(8,128)S(1)}, u32[]{:S(2)}, u32[]{:S(2)}) async-start(f32[8,96,128]{2,1,0:T(8,128)} %get-tuple-element.9), calls=%async_computation | async-start | bytes 786432 | tf_op jit(solution)/shard_map/all_to_all | solution.py:642
  8.4 11.0 %collective-permute-start = (f32[16,1024]{1,0:T(8,128)}, f32[16,1024]{1,0:T(8,128)S(1)}, u32[]{:S(2)}, u32[]{:S(2)}) collective-permute-start(f32[16,1024]{1,0:T(8,128)} %get-tuple-element.10), channel_id=1, source_target_pairs={{0,1},{1,2},{2,3},{4,5},{5,6},{6,7},{8,9},{9,10},{10,11},{12,13},{... | collective-permute-start | bytes 196616 | tf_op jit(solution)/shard_map/ppermute | solution.py:643
  11.9 7.6 %copy-start = (s32[128,1024]{1,0:T(8,128)S(1)}, s32[128,1024]{1,0:T(8,128)}, u32[]{:S(2)}) copy-start(s32[128,1024]{1,0:T(8,128)} %depth.5) | copy-start | bytes 1572868
  11.9 7.6 %copy-start.5 = (s32[1024]{0:T(1024)S(1)}, s32[1024]{0:T(1024)}, u32[]{:S(2)}) copy-start(s32[1024]{0:T(1024)} %partner.1) | copy-start | bytes 12292
  11.9 7.5 %collective-permute-start.1 = (f32[16,1024]{1,0:T(8,128)}, f32[16,1024]{1,0:T(8,128)S(1)}, u32[]{:S(2)}, u32[]{:S(2)}) collective-permute-start(f32[16,1024]{1,0:T(8,128)} %get-tuple-element.11), channel_id=1, source_target_pairs={{1,0},{2,1},{3,2},{5,4},{6,5},{7,6},{9,8},{10,9},{11,10},{13,12},{... | collective-permute-start | bytes 196616 | tf_op jit(solution)/shard_map/ppermute | solution.py:644
